TPU v7x, 32 devices: a whole 2x2x4 slice. The times are simulated.
32 devices in a mesh: rack: 4 (over z), dev: 8 (over y, x, core).
Axes of the slice: x: 2, y: 2, z: 4, core: 2. Of those that a mesh axis runs over, the one named last changes fastest.
Arguments:
- span_store: bfloat16 [704, 64, 1024], P(('rack', 'dev')), may hold values from -6 to 6
- helper_offset: int32 [22], replicated, may hold values from 1 to 31, as said below
- plane_index: int32 [64, 16], replicated, may hold values from 0 to 63, as said below
- coupling_pair: int32 [64, 11, 16], P(('rack', 'dev')), may hold values from 0 to 10
- decode_matrix: float32 [64, 4, 11], P(('rack', 'dev')), may hold values from -1.75 to 1.75
- recouple_pair: int32 [64, 64], P(('rack', 'dev')), may hold values from 0 to 63
Outputs:
- rebuilt: bfloat16 [64, 64, 1024], P(('rack', 'dev'))
Inputs may be any that keep to these rules, and one draw needn't show every extreme that they name: 22 distinct values; helper slot j of a stripe of device p is always slot j of device p + helper_offset[j] (mod the device count). `plane_index`: each row lists in increasing order the 16 indices z whose base-4 digit number y equals x, for the stripe's lost node (x, y), x below 4 and y below 3.
All inputs are finite; a program needn't handle non-finite values.
Results may differ from a plain program's by a relative error of at most 0.001.
Values may be sent and summed in bfloat16 or wider, within the bound.
No kernel may reach another device: no remote copies, remote signals or barrier semaphores. Data moves between devices by JAX's collectives and lax.ppermute only.
A program may use at most 64 MiB of HBM per device.

v0:
```python
import jax
import jax.numpy as jnp
from jax import lax
from jax.sharding import PartitionSpec as P

PLANES = 16
HELPERS = 11


COUPLING = 0.6


def composed_repair(words, decode_block, pair_block, recouple_pairs):
    stripes_here, helpers, plane_count, columns = words.shape
    group_size = decode_block.shape[1]
    helper_ids = jnp.arange(helpers, dtype=jnp.int32)
    choose = (pair_block[..., None] == helper_ids).astype(jnp.float32)
    coupled_mask = (pair_block != helper_ids[None, :, None]).astype(jnp.float32)
    identity_helpers = jnp.eye(helpers, dtype=jnp.float32)
    unmix = (identity_helpers[None, :, None, :] - COUPLING * coupled_mask[..., None] * choose) / (
        1.0 - COUPLING * COUPLING
    )
    sectioned = jnp.einsum("sth,shzg->sztg", decode_block, unmix, precision=lax.Precision.HIGHEST)
    identity_planes = jnp.eye(plane_count, dtype=jnp.float32)
    spread = jnp.einsum(
        "sztg,zy->sztgy", sectioned, identity_planes, precision=lax.Precision.HIGHEST
    )
    spread = spread.reshape(stripes_here, plane_count * group_size, helpers * plane_count)
    sub_count = plane_count * group_size
    sub_ids = jnp.arange(sub_count, dtype=jnp.int32)
    pick = (recouple_pairs[..., None] == sub_ids).astype(jnp.float32)
    distinct = (recouple_pairs != sub_ids[None, :]).astype(jnp.float32)
    mixing = jnp.eye(sub_count, dtype=jnp.float32)[None] + COUPLING * distinct[..., None] * pick
    whole = jnp.einsum("sab,sbc->sac", mixing, spread, precision=lax.Precision.HIGHEST)
    flat_words = words.reshape(stripes_here, helpers * plane_count, columns).astype(jnp.float32)
    result = jnp.einsum("sac,scw->saw", whole, flat_words, precision=lax.Precision.HIGHEST)
    return result.astype(jnp.bfloat16)


def body(span_store, helper_offset, plane_index, coupling_pair, decode_matrix, recouple_pair):
    rack_count = lax.axis_size("rack")
    dev_count = lax.axis_size("dev")
    device_count = rack_count * dev_count
    myself = lax.axis_index("rack") * dev_count + lax.axis_index("dev")
    slots = span_store.shape[0]
    sub_total = span_store.shape[1]
    per_device = slots // HELPERS
    columns = span_store.shape[-1]
    peer_ids = jnp.arange(device_count, dtype=jnp.int32)
    wanted = (myself - peer_ids) % device_count
    matches = (wanted[:, None] == helper_offset[None, :]).astype(jnp.int32)
    slot_of = jnp.argmax(matches, axis=1)
    stripe_ids = peer_ids * per_device + slot_of // HELPERS
    planes = plane_index[stripe_ids]
    flat_rows = span_store.reshape(slots * sub_total, columns)
    row_index = (slot_of[:, None] * sub_total + planes).reshape(-1)
    outgoing = jnp.take(flat_rows, row_index, axis=0).reshape(device_count, PLANES, columns)
    sources = (myself + helper_offset) % device_count
    arrived = lax.all_to_all(outgoing, ("rack", "dev"), split_axis=0, concat_axis=0, tiled=True)
    piece_columns = arrived.shape[-1]
    words = jnp.take(arrived, sources, axis=0).reshape(per_device, HELPERS, PLANES, piece_columns)
    return composed_repair(words, decode_matrix, coupling_pair, recouple_pair)


def solution(mesh):
    placed = (
        P(("rack", "dev"), None, None),
        P(),
        P(),
        P(("rack", "dev"), None, None),
        P(("rack", "dev"), None, None),
        P(("rack", "dev"), None),
    )
    return jax.shard_map(
        body, mesh=mesh, in_specs=placed, out_specs=P(("rack", "dev"), None, None), check_vma=False
    )
```

profile of v0, /device:TPU:0, one launch (start us, length us, event | category | flops | bytes accessed | tf_op | source)
XLA Modules:
  0.0 47.1 jit_solution(411024563035177864)
XLA Ops:
  0.0 1.4 %iota_reduce_fusion = (s32[32]{0:T(128)}, s32[32]{0:T(128)S(1)}) fusion(s32[32]{0:T(128)S(1)} %and_select_fusion.1, s32[22]{0:T(128)} %param.7), kind=kLoop, calls=%fused_computation.30 | loop fusion | flops 6112 | bytes 472 | tf_op jit(solution)/shard_map/body/reduce | solution.py:52
  1.5 0.8 %copy.18 = s32[64,16]{1,0:T(8,128)S(1)} copy(s32[64,16]{0,1:T(8,128)} %param.8) | data formatting | bytes 8192 | tf_op args[2]
  2.2 0.6 %gather_fusion = s32[32,16]{1,0:T(8,128)S(1)} fusion(s32[64,16]{1,0:T(8,128)S(1)} %copy.18, s32[1024]{0:T(1024)S(1)} %pad_clamp_fusion.2), kind=kCustom, calls=%fused_computation | custom fusion | bytes 4224 | tf_op jit(solution)/shard_map/gather | solution.py:54
  2.8 0.1 compare_and_fusion
  2.9 0.1 add.103
  3.0 0.0 copy-done
  3.0 2.8 %gather_fusion.1 = bf16[512,1024]{1,0:T(8,128)(2,1)} fusion(bf16[1408,1024]{1,0:T(8,128)(2,1)S(1)} %bitcast.18, s32[1024]{0:T(1024)S(1)} %pad_clamp_fusion.1), kind=kCustom, calls=%fused_computation.1 | custom fusion | bytes 2099200 | tf_op jit(solution)/shard_map/jit(_take)/gather | solution.py:57
  5.8 2.5 %broadcast_select_fusion = bf16[32,16,1024]{2,1,0:T(8,128)(2,1)} fusion(bf16[32,16,1024]{2,1,0:T(8,128)(2,1)} %bitcast.19, pred[32,16]{1,0:T(8,128)(4,1)S(1)} %get-tuple-element.9), kind=kLoop, calls=%fused_computation.6 | loop fusion | flops 524288 | bytes 2097664 | tf_op jit(solution)/shard_map/jit(_take)/select_n | solution.py:57
  8.3 7.5 %all-to-all-start = ((bf16[32,16,1024]{2,1,0:T(8,128)(2,1)}), bf16[32,16,1024]{2,1,0:T(8,128)(2,1)}, u32[]{:S(2)}, u32[]{:S(2)}) async-start(bf16[32,16,1024]{2,1,0:T(8,128)(2,1)} %broadcast_select_fusion), calls=%async_computation | async-start | bytes 2097152 | tf_op jit(solution)/shard_map/all_to_all | solution.py:59
  15.7 0.0 copy-done.3
  15.8 0.1 broadcast_in_dim.44
  15.8 0.1 broadcast_in_dim.45
  15.9 0.1 broadcast_in_dim.46
  16.0 0.0 copy-done.1
  16.1 0.0 copy-done.4
  16.1 0.3 convolution_bitcast_fusion
  16.4 0.1 copy.17
  16.5 1.3 %multiply_bitcast_fusion = f32[2,16,4,11,16]{4,3,2,1,0:T(8,128)} fusion(f32[16,2,4,11]{3,2,0,1:T(4,128)S(1)} %copy.17, f32[16,16]{1,0:T(8,128)S(1)} %fusion.16), kind=kLoop, calls=%fused_computation.5 | loop fusion | flops 22528 | bytes 96768 | tf_op jit(solution)/shard_map/sztg,zy->sztgy/transpose | solution.py:25
  17.8 1.5 %reshape.100 = f32[2,64,176]{2,1,0:T(8,128)S(1)} reshape(f32[2,16,4,11,16]{4,3,2,1,0:T(8,128)} %multiply_bitcast_fusion) | data formatting | bytes 180224 | tf_op jit(solution)/shard_map/reshape | solution.py:28
  19.4 0.3 fusion.8
  19.7 22.2 %all-to-all-done = bf16[32,16,1024]{2,1,0:T(8,128)(2,1)} async-done(((bf16[32,16,1024]{2,1,0:T(8,128)(2,1)}), bf16[32,16,1024]{2,1,0:T(8,128)(2,1)}, u32[]{:S(2)}, u32[]{:S(2)}) %all-to-all-start) | async-done | bytes 1048608 | tf_op jit(solution)/shard_map/all_to_all | solution.py:59
  41.9 2.7 %gather_fusion.2 = bf16[22,16,1024]{2,1,0:T(8,128)(2,1)} fusion(bf16[32,16,1024]{2,1,0:T(8,128)(2,1)} %all-to-all-done, s32[1024]{0:T(1024)S(1)} %pad_clamp_fusion), kind=kCustom, calls=%fused_computation.2 | custom fusion | bytes 1441880 | tf_op jit(solution)/shard_map/jit(_take)/gather | solution.py:61
  44.6 1.2 %bitcast_select_fusion = bf16[2,176,1024]{2,1,0:T(8,128)(2,1)S(1)} fusion(pred[2,176]{1,0:T(4,128)(4,1)S(1)} %broadcast_in_dim.46, bf16[2,176,1024]{2,1,0:T(8,128)(2,1)} %bitcast.20), kind=kLoop, calls=%fused_computation.7 | loop fusion | flops 360448 | bytes 1442144 | tf_op jit(solution)/shard_map/jit(_take)/select_n | solution.py:61
  45.9 1.2 %convolution_convert_fusion = bf16[2,64,1024]{2,1,0:T(8,128)(2,1)} fusion(f32[2,64,176]{2,1,0:T(8,128)S(1)} %fusion.8, bf16[2,176,1024]{2,1,0:T(8,128)(2,1)S(1)} %bitcast_select_fusion), kind=kOutput, calls=%fused_computation.3 | convolution fusion | flops 276955136 | bytes 1073152 | tf_op jit(solution)/shard_map/sac,scw->saw/dot_general | solution.py:36
  (20 shorter events, 0.1 us)
Async XLA Ops:
  0.0 3.0 %copy-start = (bf16[22,64,1024]{2,1,0:T(8,128)(2,1)S(1)}, bf16[22,64,1024]{2,1,0:T(8,128)(2,1)}, u32[]{:S(2)}) copy-start(bf16[22,64,1024]{2,1,0:T(8,128)(2,1)} %param.6) | copy-start | bytes 8650756
  5.8 9.9 %copy-start.3 = (s32[22]{0:T(128)S(1)}, s32[22]{0:T(128)}, u32[]{:S(2)}) copy-start(s32[22]{0:T(128)} %param.7) | copy-start | bytes 268
  5.8 10.2 %copy-start.1 = (s32[2,11,16]{2,0,1:T(2,128)S(1)}, s32[2,11,16]{2,0,1:T(2,128)}, u32[]{:S(2)}) copy-start(s32[2,11,16]{2,0,1:T(2,128)} %param.9) | copy-start | bytes 4228
  5.8 10.3 %copy-start.4 = (f32[2,4,11]{2,1,0:T(4,128)S(1)}, f32[2,4,11]{2,1,0:T(4,128)}, u32[]{:S(2)}) copy-start(f32[2,4,11]{2,1,0:T(4,128)} %param.10) | copy-start | bytes 1060
  8.3 11.1 %copy-start.2 = (s32[2,64]{1,0:T(2,128)S(1)}, s32[2,64]{1,0:T(2,128)}, u32[]{:S(2)}) copy-start(s32[2,64]{1,0:T(2,128)} %param.11) | copy-start | bytes 1540
  8.3 33.6 %all-to-all-start = ((bf16[32,16,1024]{2,1,0:T(8,128)(2,1)}), bf16[32,16,1024]{2,1,0:T(8,128)(2,1)}, u32[]{:S(2)}, u32[]{:S(2)}) async-start(bf16[32,16,1024]{2,1,0:T(8,128)(2,1)} %broadcast_select_fusion), calls=%async_computation | async-start | bytes 2097152 | tf_op jit(solution)/shard_map/all_to_all | solution.py:59
where the time goes:
time: 47.5 us; the launch traced here: 47.1 us
  waiting for transfers between devices  22.2 us (47%)
  local copies, waits for them, and re-layouts  8.9 us (19%)
  starting transfers between devices  7.45 us (16%)
  other arithmetic  6.62 us (14%)
  matrix products  1.83 us (4%)
    all_to_all x1, waiting for transfers between devices, body(): lax.all_to_all(outgoing, ('rack', 'dev'), split_axis=0, concat_axis=0, ti...  22.2 us
    all_to_all x1, starting transfers between devices, body(): lax.all_to_all(outgoing, ('rack', 'dev'), split_axis=0, concat_axis=0, ti...  7.45 us
    gather x1, local copies, waits for them, and re-layouts, body(): jnp.take(flat_rows, row_index, axis=0)  2.79 us
    gather x1, local copies, waits for them, and re-layouts, body(): jnp.take(arrived, sources, axis=0)  2.73 us
    select_n x2, other arithmetic, body(): jnp.take(flat_rows, row_index, axis=0)  2.47 us
    reshape x1, local copies, waits for them, and re-layouts, composed_repair(): spread.reshape(stripes_here, plane_count * group_size, helpers * plane_co...  1.53 us
    another operation x1, other arithmetic, body(): slot_of = jnp.argmax(matches, axis=1)  1.41 us
    transpose x1, other arithmetic, composed_repair(): jnp.einsum('sztg,zy->sztgy', sectioned, identity_planes, precision=lax.Pr...  1.32 us
  transfers between devices with their start and end apart: 1, of which 1 were waited for; matrix products, arithmetic and copies ran while one was open for 8% of the time, Pallas kernels for 0%

commit v1 on v0

v1 whole, which is shorter than its diff:
```python
import jax
import jax.numpy as jnp
from jax import lax
from jax.sharding import PartitionSpec as P

COUPLING = 0.6
HIGHEST = lax.Precision.HIGHEST


def repair_matrix(decode_block, pair_block, recouple_pairs, sources, device_count):
    stripes_here, helpers, plane_count = pair_block.shape
    group_size = decode_block.shape[1]
    helper_ids = jnp.arange(helpers, dtype=jnp.int32)
    choose = (pair_block[..., None] == helper_ids).astype(jnp.float32)
    coupled = (pair_block != helper_ids[None, :, None]).astype(jnp.float32)
    unmix = (jnp.eye(helpers, dtype=jnp.float32)[None, :, None, :] - COUPLING * coupled[..., None] * choose) / (
        1.0 - COUPLING * COUPLING
    )
    sectioned = jnp.einsum("sth,shzg->sztg", decode_block, unmix, precision=HIGHEST)
    sub_count = plane_count * group_size
    rows_in = jnp.arange(device_count * plane_count, dtype=jnp.int32)
    at_row = (sources.reshape(stripes_here, helpers)[..., None] == rows_in // plane_count).astype(jnp.float32)
    spread = jnp.einsum(
        "sag,sgr->sar", sectioned.reshape(stripes_here, sub_count, helpers), at_row, precision=HIGHEST
    )
    same_plane = jnp.arange(sub_count, dtype=jnp.int32)[:, None] // group_size == rows_in[None, :] % plane_count
    spread = jnp.where(same_plane[None], spread, 0.0)
    sub_ids = jnp.arange(sub_count, dtype=jnp.int32)
    pick = (recouple_pairs[..., None] == sub_ids).astype(jnp.float32)
    distinct = (recouple_pairs != sub_ids[None, :]).astype(jnp.float32)
    mixing = jnp.eye(sub_count, dtype=jnp.float32)[None] + COUPLING * distinct[..., None] * pick
    whole = jnp.einsum("sab,sbc->sac", mixing, spread, precision=HIGHEST)
    return whole.reshape(stripes_here * sub_count, device_count * plane_count)


def body(span_store, helper_offset, plane_index, coupling_pair, decode_matrix, recouple_pair):
    dev_count = lax.axis_size("dev")
    device_count = lax.axis_size("rack") * dev_count
    myself = lax.axis_index("rack") * dev_count + lax.axis_index("dev")
    slots, sub_total, columns = span_store.shape
    stripes_here, helpers, plane_count = coupling_pair.shape
    sub_count = recouple_pair.shape[1]
    peer_ids = jnp.arange(device_count, dtype=jnp.int32)
    slot_ids = jnp.arange(slots, dtype=jnp.int32)
    wanted = (myself - peer_ids) % device_count
    slot_of = jnp.sum(jnp.where(wanted[:, None] == helper_offset[None, :], slot_ids[None, :], 0), axis=1)
    stripe_of = slot_of // helpers
    at_stripe = (stripe_of[:, None] == jnp.arange(stripes_here, dtype=jnp.int32)).astype(jnp.int32)
    planes = jnp.sum(
        plane_index.reshape(device_count, stripes_here, plane_count) * at_stripe[..., None], axis=1
    )
    flat_rows = span_store.reshape(slots * sub_total, columns)
    row_index = (slot_of[:, None] * sub_total + planes).reshape(-1)
    outgoing = jnp.take(flat_rows, row_index, axis=0, mode="clip").reshape(device_count, plane_count, columns)
    arrived = lax.all_to_all(outgoing, ("rack", "dev"), split_axis=0, concat_axis=0, tiled=True)
    sources = (myself + helper_offset) % device_count
    whole = repair_matrix(decode_matrix, coupling_pair, recouple_pair, sources, device_count)
    rows = arrived.reshape(device_count * plane_count, columns)
    result = jnp.dot(whole, rows.astype(jnp.float32), precision=HIGHEST)
    return result.astype(jnp.bfloat16).reshape(stripes_here, sub_count, columns)


def solution(mesh):
    split = ("rack", "dev")
    placed = (
        P(split, None, None),
        P(),
        P(),
        P(split, None, None),
        P(split, None, None),
        P(split, None),
    )
    return jax.shard_map(body, mesh=mesh, in_specs=placed, out_specs=P(split, None, None), check_vma=False)
```

time: 47.5 us -> 41.3 us (0.87)
  other arithmetic: 6.62 us -> 1.32 us
  local copies, waits for them, and re-layouts: 8.9 us -> 3.89 us
  waiting for transfers between devices: 22.2 us -> 24.7 us
  matrix products: 1.83 us -> 3.56 us
    select_n x3 -> x4, other arithmetic: 3.71 us -> 0.02 us  [the longest x1 0.01 us: body(): sources = (myself + helper_offset) % device_count]
    gather x3 -> x1, local copies, waits for them, and re-layouts: 6.1 us -> 2.78 us  [body(): jnp.take(flat_rows, row_index, axis=0, mode='clip')]
    all_to_all x1, waiting for transfers between devices: 22.2 us -> 24.7 us  [body(): lax.all_to_all(outgoing, ('rack', 'dev'), split_axis=0, concat_axis=0, ti...]
    dot_general x3 -> x4, matrix products: 1.83 us -> 3.56 us  [the longest x1 2.52 us: body(): result = jnp.dot(whole, rows.astype(jnp.float32), precision=HIGHEST)]
    reshape x1 -> x0, local copies, waits for them, and re-layouts: 1.53 us -> none  [composed_repair(): spread.reshape(stripes_here, plane_count * group_size, helpers * plane_co...]
    another operation x2 -> x0, other arithmetic: 1.42 us -> none  [the longest x1 1.41 us: body(): slot_of = jnp.argmax(matches, axis=1)]
    transpose x1 -> x0, other arithmetic: 1.32 us -> none  [composed_repair(): jnp.einsum('sztg,zy->sztgy', sectioned, identity_planes, precision=lax.Pr...]
    reduce_sum x0 -> x2, other arithmetic: none -> 1.01 us  [the longest x1 0.9 us: body(): jnp.sum(jnp.where(wanted[:, None] == helper_offset[None, :], slot_ids[Non...]
  transfers between devices with their start and end apart: 1 -> 1, of which waited for: 1 -> 1; matrix products, arithmetic and copies ran while one was open for 8% -> 3% of each run, Pallas kernels for 0% -> 0%
where the time goes in v1:
time: 41.3 us; the launch traced here: 41.1 us
  waiting for transfers between devices  24.7 us (60%)
  starting transfers between devices  7.45 us (18%)
  local copies, waits for them, and re-layouts  3.89 us (9%)
  matrix products  3.56 us (9%)
  other arithmetic  1.32 us (3%)
    all_to_all x1, waiting for transfers between devices, body(): lax.all_to_all(outgoing, ('rack', 'dev'), split_axis=0, concat_axis=0, ti...  24.7 us
    all_to_all x1, starting transfers between devices, body(): lax.all_to_all(outgoing, ('rack', 'dev'), split_axis=0, concat_axis=0, ti...  7.45 us
    gather x1, local copies, waits for them, and re-layouts, body(): jnp.take(flat_rows, row_index, axis=0, mode='clip')  2.78 us
    dot_general x1, matrix products, body(): result = jnp.dot(whole, rows.astype(jnp.float32), precision=HIGHEST)  2.52 us
    reduce_sum x1, other arithmetic, body(): jnp.sum(jnp.where(wanted[:, None] == helper_offset[None, :], slot_ids[Non...  0.9 us
  transfers between devices with their start and end apart: 1, of which 1 were waited for; matrix products, arithmetic and copies ran while one was open for 3% of the time, Pallas kernels for 0%

profile of v1, /device:TPU:0, one launch (start us, length us, event | category | flops | bytes accessed | tf_op | source)
XLA Modules:
  0.0 41.1 jit_solution(11095585924655746839)
XLA Ops:
  0.0 0.0 copy-start
  0.0 0.9 %select_reduce_fusion = s32[32]{0:T(128)S(1)} fusion(s32[32]{0:T(128)S(1)} %and_select_fusion.1, s32[22]{0:T(128)} %param.7), kind=kLoop, calls=%fused_computation.31 | loop fusion | flops 2080 | bytes 344 | tf_op jit(solution)/shard_map/reduce_sum | solution.py:46
  0.9 0.1 fusion.19
  1.0 0.8 %copy.17 = s32[64,16]{1,0:T(8,128)S(1)} copy(s32[64,16]{0,1:T(8,128)} %param.8) | data formatting | bytes 8192 | tf_op args[2]
  1.8 0.1 multiply_reduce_fusion
  1.9 0.1 broadcast_add_fusion
  2.0 0.1 reshape.218
  2.1 0.0 copy-done
  2.1 0.0 copy-start.4
  2.1 0.0 copy-start.1
  2.1 0.0 copy-start.3
  2.1 0.0 copy-start.2
  2.1 2.8 %gather_fusion = bf16[512,1024]{1,0:T(8,128)(2,1)} fusion(bf16[1408,1024]{1,0:T(8,128)(2,1)S(1)} %bitcast.18, s32[1024]{0:T(1024)S(1)} %pad_clamp_fusion), kind=kCustom, calls=%fused_computation | custom fusion | bytes 2099200 | tf_op jit(solution)/shard_map/jit(_take)/gather | solution.py:54
  4.9 7.5 %all-to-all-start = ((bf16[32,16,1024]{2,1,0:T(8,128)(2,1)}), bf16[32,16,1024]{2,1,0:T(8,128)(2,1)}, u32[]{:S(2)}, u32[]{:S(2)}) async-start(bf16[32,16,1024]{2,1,0:T(8,128)(2,1)} %bitcast.19), calls=%async_computation | async-start | bytes 2097152 | tf_op jit(solution)/shard_map/all_to_all | solution.py:55
  12.4 0.0 copy-done.4
  12.4 0.1 eq.119
  12.5 0.0 copy-done.3
  12.5 0.3 convolution_bitcast_fusion
  12.8 0.1 copy.15
  13.0 0.1 broadcast_compare_fusion
  13.1 0.3 convolution_select_fusion
  13.5 0.4 %fusion.8 = f32[2,64,512]{2,1,0:T(8,128)S(1)} fusion(f32[2,64,512]{2,1,0:T(8,128)S(1)} %convolution_select_fusion, f32[2,64]{1,0:T(2,128)S(1)} %compare_select_fusion.5, s32[2,64]{1,0:T(2,128)S(1)} %copy-done.2, f32[64,64]{1,0:T(8,128)S(1)} %fusion.18), kind=kOutput, calls=%fused_computation.14 | convolution fusion | flops 50356224 | bytes 541696 | tf_op jit(solution)/shard_map/sab,sbc->sac/dot_general | solution.py:32
  13.9 24.7 %all-to-all-done = bf16[32,16,1024]{2,1,0:T(8,128)(2,1)} async-done(((bf16[32,16,1024]{2,1,0:T(8,128)(2,1)}), bf16[32,16,1024]{2,1,0:T(8,128)(2,1)}, u32[]{:S(2)}, u32[]{:S(2)}) %all-to-all-start) | async-done | bytes 1048608 | tf_op jit(solution)/shard_map/all_to_all | solution.py:55
  38.5 2.5 %convolution_convert_fusion = bf16[128,1024]{1,0:T(8,128)(2,1)} fusion(f32[128,512]{1,0:T(8,128)S(1)} %bitcast.20, bf16[512,1024]{1,0:T(8,128)(2,1)} %bitcast.8), kind=kOutput, calls=%fused_computation.1 | convolution fusion | flops 805437440 | bytes 1572864 | tf_op jit(solution)/shard_map/dot_general | solution.py:59
  (15 shorter events, 0.1 us)
Async XLA Ops:
  0.0 2.1 %copy-start = (bf16[22,64,1024]{2,1,0:T(8,128)(2,1)S(1)}, bf16[22,64,1024]{2,1,0:T(8,128)(2,1)}, u32[]{:S(2)}) copy-start(bf16[22,64,1024]{2,1,0:T(8,128)(2,1)} %param.6) | copy-start | bytes 8650756
  2.1 10.3 %copy-start.4 = (s32[22]{0:T(128)S(1)}, s32[22]{0:T(128)}, u32[]{:S(2)}) copy-start(s32[22]{0:T(128)} %param.7) | copy-start | bytes 268
  2.1 10.4 %copy-start.1 = (s32[2,11,16]{2,0,1:T(2,128)S(1)}, s32[2,11,16]{2,0,1:T(2,128)}, u32[]{:S(2)}) copy-start(s32[2,11,16]{2,0,1:T(2,128)} %param.9) | copy-start | bytes 4228
  2.1 10.4 %copy-start.3 = (f32[2,4,11]{2,1,0:T(4,128)S(1)}, f32[2,4,11]{2,1,0:T(4,128)}, u32[]{:S(2)}) copy-start(f32[2,4,11]{2,1,0:T(4,128)} %param.10) | copy-start | bytes 1060
  2.1 10.9 %copy-start.2 = (s32[2,64]{1,0:T(2,128)S(1)}, s32[2,64]{1,0:T(2,128)}, u32[]{:S(2)}) copy-start(s32[2,64]{1,0:T(2,128)} %param.11) | copy-start | bytes 1540
  4.9 33.6 %all-to-all-start = ((bf16[32,16,1024]{2,1,0:T(8,128)(2,1)}), bf16[32,16,1024]{2,1,0:T(8,128)(2,1)}, u32[]{:S(2)}, u32[]{:S(2)}) async-start(bf16[32,16,1024]{2,1,0:T(8,128)(2,1)} %bitcast.19), calls=%async_computation | async-start | bytes 2097152 | tf_op jit(solution)/shard_map/all_to_all | solution.py:55
